TPU v7x, 128 devices: a whole 4x4x4 slice. The times are simulated.
128 devices in a mesh: ctx: 8 (over x, z_lo), head: 16 (over z_hi, y, core).
Axes of the slice: x: 4, y: 4, z: 4 (z_hi: 2, z_lo: 2; z = z_hi * 2 + z_lo), core: 2. Of those that a mesh axis runs over, the one named last changes fastest.
Arguments:
- queries: bfloat16 [256, 16384], P(None, 'head'), may hold values from -64 to 64, as said below
- grad_out: bfloat16 [256, 16384], P(None, 'head'), may hold values from -24 to 24
- latent: bfloat16 [16384, 512], P(('ctx', 'head')), may hold values from -6.1 to 6.1
- up_key: bfloat16 [512, 16384], P(None, 'head'), as said below
- up_value: bfloat16 [512, 16384], P(None, 'head'), may hold values from -0.25 to 0.25
Outputs:
- grad_queries: float32 [256, 16384], P('ctx', 'head')
- grad_latent: float32 [16384, 512], P(('ctx', 'head'))
- grad_up_key: float32 [512, 16384], P('ctx', 'head')
- grad_up_value: float32 [512, 16384], P('ctx', 'head')
Inputs may be any that keep to these rules, and one draw needn't show every extreme that they name: `queries`: entries lie within 64 in magnitude. `up_key`: entries lie within 4 / sqrt(512) in magnitude.
All inputs are finite; a program needn't handle non-finite values.
Results may differ from a plain program's by a relative error of at most 0.005.
Values may be sent and summed in bfloat16 or wider, within the bound.
A program may use at most 128 MiB of HBM per device.

v0:
```python
import math
import jax
import jax.numpy as jnp
from jax import lax
from jax.sharding import PartitionSpec as P

HD = 128


def joined(part, axis, combine):
    gathered = jax.tree.map(lambda a: lax.all_gather(a, axis), part)

    def take(source):
        return jax.tree.map(lambda a: lax.dynamic_index_in_dim(a, source, 0, False), gathered)

    return lax.fori_loop(
        1, lax.axis_size(axis), lambda source, state: combine(state, take(source)), take(0)
    )


def join_pairs(former, latter):
    maxima = jnp.maximum(former[0], latter[0])
    left_factor = jnp.exp(former[0] - maxima)
    right_factor = jnp.exp(latter[0] - maxima)
    return (maxima, former[1] * left_factor + latter[1] * right_factor)


def local(queries, grad_out, latent, up_key, up_value):
    scale = 1.0 / math.sqrt(HD)
    local_heads = queries.shape[1] // HD
    width = queries.shape[1]
    query_count = queries.shape[0]
    contract_cols = (((1,), (1,)), ((), ()))
    contract_rows = (((0,), (0,)), ((), ()))
    block = lax.all_gather(latent, "head", axis=0, tiled=True)
    key_rows = block.shape[0]
    total_len = key_rows * lax.axis_size("ctx")
    first_key = lax.axis_index("ctx") * key_rows
    key_block = jnp.dot(block, up_key, preferred_element_type=jnp.float32)
    value_block = jnp.dot(block, up_value, preferred_element_type=jnp.float32).astype(jnp.bfloat16)
    query_pos = total_len - query_count + lax.iota(jnp.int32, query_count)
    key_pos = first_key + lax.iota(jnp.int32, key_rows)
    visible = key_pos[None, :] <= query_pos[:, None]
    head_ids = jnp.arange(local_heads, dtype=jnp.int32)

    def head_inputs(head_index):
        offset = head_index * HD
        return (
            lax.dynamic_slice_in_dim(queries, offset, HD, 1),
            lax.dynamic_slice_in_dim(grad_out, offset, HD, 1),
            lax.dynamic_slice_in_dim(key_block, offset, HD, 1),
            lax.dynamic_slice_in_dim(value_block, offset, HD, 1),
        )

    def masked_scores(query_head, key_head):
        raw = (
            lax.dot_general(
                query_head.astype(jnp.float32),
                key_head,
                contract_cols,
                precision=lax.Precision.HIGHEST,
            )
            * scale
        )
        return jnp.where(visible, raw, -jnp.inf)

    def product_scores(grad_head, value_head):
        return lax.dot_general(
            grad_head, value_head, contract_cols, preferred_element_type=jnp.float32
        )

    def pick_row(table, head_index):
        return lax.dynamic_index_in_dim(table, head_index, 0, keepdims=False)

    def local_pair(head_index):
        query_head, grad_head, key_head, value_head = head_inputs(head_index)
        scores = masked_scores(query_head, key_head)
        maxima = jnp.max(scores, axis=1)
        return (maxima, jnp.sum(jnp.exp(scores - maxima[:, None]), axis=1))

    local_max, local_sum = lax.map(local_pair, head_ids)
    maxima, totals = joined((local_max, local_sum), "ctx", join_pairs)

    def local_delta(head_index):
        query_head, grad_head, key_head, value_head = head_inputs(head_index)
        scores = masked_scores(query_head, key_head)
        probs = (
            jnp.exp(scores - pick_row(maxima, head_index)[:, None])
            / pick_row(totals, head_index)[:, None]
        )
        return jnp.sum(probs * product_scores(grad_head, value_head), axis=1)

    deltas = lax.psum(lax.map(local_delta, head_ids), "ctx")

    def accumulate(head_index, carry):
        query_acc, grad_kv = carry
        query_head, grad_head, key_head, value_head = head_inputs(head_index)
        scores = masked_scores(query_head, key_head)
        probs = (
            jnp.exp(scores - pick_row(maxima, head_index)[:, None])
            / pick_row(totals, head_index)[:, None]
        )
        grad_probs = product_scores(grad_head, value_head)
        grad_scores = (probs * (grad_probs - pick_row(deltas, head_index)[:, None]) * scale).astype(
            jnp.bfloat16
        )
        query_part = jnp.dot(
            grad_scores.astype(jnp.float32), key_head, precision=lax.Precision.HIGHEST
        )
        key_grad = lax.dot_general(
            grad_scores, query_head, contract_rows, preferred_element_type=jnp.float32
        ).astype(jnp.bfloat16)
        value_grad = lax.dot_general(
            probs.astype(jnp.bfloat16), grad_head, contract_rows, preferred_element_type=jnp.float32
        ).astype(jnp.bfloat16)
        offset = head_index * HD
        anchor = jnp.zeros((), jnp.int32)
        query_acc = lax.dynamic_update_slice(query_acc, query_part, (anchor, offset))
        grad_kv = lax.dynamic_update_slice(grad_kv, key_grad, (anchor, offset))
        grad_kv = lax.dynamic_update_slice(grad_kv, value_grad, (anchor, width + offset))
        return (query_acc, grad_kv)

    start_state = (
        jnp.zeros((query_count, width), jnp.float32),
        jnp.zeros((key_rows, 2 * width), jnp.bfloat16),
    )
    query_acc, grad_kv = lax.fori_loop(0, local_heads, accumulate, start_state)
    up_both = jnp.concatenate([up_key, up_value], axis=1)
    grad_queries = lax.psum_scatter(query_acc, "ctx", scatter_dimension=0, tiled=True)
    weight_sums = lax.psum_scatter(
        lax.dot_general(block, grad_kv, contract_rows, preferred_element_type=jnp.float32),
        "ctx",
        scatter_dimension=0,
        tiled=True,
    )
    own_rows = latent.shape[0]
    summed = lax.psum(
        lax.dot_general(grad_kv, up_both, contract_cols, preferred_element_type=jnp.float32), "head"
    )
    grad_latent = lax.dynamic_slice_in_dim(summed, lax.axis_index("head") * own_rows, own_rows, 0)
    return (grad_queries, grad_latent, weight_sums[:, :width], weight_sums[:, width:])


def solution(mesh):
    return jax.shard_map(
        local,
        mesh=mesh,
        in_specs=(
            P(None, "head"),
            P(None, "head"),
            P(("ctx", "head"), None),
            P(None, "head"),
            P(None, "head"),
        ),
        out_specs=(P("ctx", "head"), P(("ctx", "head"), None), P("ctx", "head"), P("ctx", "head")),
        check_vma=False,
    )
```

profile of v0, /device:TPU:0, one launch (start us, length us, event | category | flops | bytes accessed | tf_op | source)
XLA Modules:
  0.0 633.1 jit_solution(3696228629027708976)
XLA Ops:
  8.0 53.2 %all-gather.4.cloned.1.call-done = bf16[2048,512]{1,0:T(8,128)(2,1)} async-done(((bf16[128,512]{1,0:T(8,128)(2,1)}), bf16[2048,512]{1,0:T(8,128)(2,1)}) %all-gather.4.cloned.1.call-update) | async-done | bytes 2097168 | tf_op jit(solution)/shard_map/all_gather | solution.py:35
  61.2 7.4 %fusion.52 = f32[2048,1024]{1,0:T(8,128)} fusion(bf16[2048,512]{1,0:T(8,128)(2,1)} %all-gather.4.cloned.1.call-done, bf16[512,1024]{1,0:T(8,128)(2,1)} %param.16), kind=kOutput, calls=%fused_computation.71 | convolution fusion | flops 2147483648 | bytes 11534336 | tf_op jit(solution)/shard_map/dot_general | solution.py:39
  68.6 34.9 %while.60 = (s32[]{:T(128)}, f32[8,256]{1,0:T(8,128)S(1)}, f32[8,256]{1,0:T(8,128)S(1)}, s32[8]{0:T(128)S(1)}, bf16[256,1024]{1,0:T(8,128)(2,1)S(1)}, /*index=5*...) while((s32[]{:T(128)}, f32[8,256]{1,0:T(8,128)S(1)}, ...), condition=%wide.region_3.4_spmd.clone, body=%wide.region_0.3_spmd.clone.sunk | while | flops 808451584 | bytes 5326015 | solution.py:81
  103.6 28.2 %all-gather.1 = f32[64,256]{1,0:T(8,128)S(1)} all-gather(f32[8,256]{1,0:T(8,128)S(1)} %get-tuple-element.493), channel_id=3, replica_groups=mesh['ctx'=8,'head'=16] {'ctx'}, dimensions={0}, use_global_device_ids=true | all-gather | bytes 73728 | tf_op jit(solution)/shard_map/all_gather | solution.py:11
  131.8 28.2 %all-gather = f32[64,256]{1,0:T(8,128)S(1)} all-gather(f32[8,256]{1,0:T(8,128)S(1)} %get-tuple-element.492), channel_id=2, replica_groups=mesh['ctx'=8,'head'=16] {'ctx'}, dimensions={0}, use_global_device_ids=true | all-gather | bytes 73728 | tf_op jit(solution)/shard_map/all_gather | solution.py:11
  160.2 5.9 convolution_convert_fusion.2
  166.1 60.3 %while.61 = (s32[]{:T(128)}, f32[8,256]{1,0:T(8,128)S(1)}, s32[8]{0:T(128)S(1)}, bf16[256,1024]{1,0:T(8,128)(2,1)S(1)}, f32[2048,1024]{1,0:T(8,128)}, /*index=5*...) while((s32[]{:T(128)}, f32[8,256]{1,0:T(8,128)S(1)}, ...), condition=%wide.region_8.9_spmd.clone, body=%wide.region_6.8_spmd.clone.sunk | while | flops 943193856 | bytes 5918977 | solution.py:93
  226.5 19.1 %psum.14 = f32[8,256]{1,0:T(8,128)S(1)} all-reduce(f32[8,256]{1,0:T(8,128)S(1)} %get-tuple-element.496), channel_id=1, replica_groups=mesh['ctx'=8,'head'=16] {'ctx'}, use_global_device_ids=true, to_apply=%region_9.10 | all-reduce | flops 2048 | bytes 16384 | tf_op jit(solution)/shard_map/psum | solution.py:93
  245.7 4.3 broadcast_in_dim.48
  250.0 80.9 %while.62 = (s32[]{:T(128)}, f32[256,1024]{1,0:T(8,128)S(1)}, bf16[2048,2048]{1,0:T(8,128)(2,1)}, bf16[256,1024]{1,0:T(8,128)(2,1)S(1)}, f32[2048,1024]{1,0:T(8,...) while((s32[]{:T(128)}, f32[256,1024]{1,0:T(8,128)S(1)}, ...), condition=%wide.region_11.12_spmd.clone, body=%wide.region_10.11_spmd.clone.sunk | while | flops 2019033088 | bytes 13522222 | solution.py:127
  250.0 2.8 fusion.102
  260.2 2.7 fusion.102
  270.3 2.7 fusion.102
  280.4 2.7 fusion.102
  290.5 2.7 fusion.102
  300.6 2.7 fusion.102
  310.7 2.7 fusion.102
  320.8 2.7 fusion.102
  330.9 10.5 %fusion.45 = f32[2048,512]{1,0:T(8,128)} fusion(bf16[2048,2048]{1,0:T(8,128)(2,1)} %get-tuple-element.498, bf16[512,1024]{1,0:T(8,128)(2,1)} %param.17, bf16[512,1024]{1,0:T(8,128)(2,1)S(1)} %copy-done.3), kind=kOutput, calls=%fused_computation.61 | convolution fusion | flops 4299161600 | bytes 14680064 | tf_op jit(solution)/shard_map/dot_general | solution.py:138
  343.0 9.8 %convolution_bitcast_fusion = f32[512,2048]{0,1:T(8,128)} fusion(bf16[2048,2048]{1,0:T(8,128)(2,1)} %get-tuple-element.498, bf16[2048,512]{1,0:T(8,128)(2,1)S(1)} %copy-done.2), kind=kOutput, calls=%fused_computation.60 | convolution fusion | flops 4294967296 | bytes 14680064 | tf_op jit(solution)/shard_map/dot_general | solution.py:131
  352.8 5.5 copy.13
  358.8 130.5 %all-reduce.2.cloned.1.call-done = f32[2048,512]{1,0:T(8,128)} async-done(((f32[2048,512]{1,0:T(8,128)}), f32[2048,512]{1,0:T(8,128)}) %all-reduce.2.cloned.1.call-update) | async-done | bytes 4194320 | tf_op jit(solution)/shard_map/psum | solution.py:137
  491.1 91.7 %reduce-scatter.7.cloned.1.call-done = f32[64,2048]{1,0:T(8,128)} async-done(((f32[512,2048]{1,0:T(8,128)}), f32[64,2048]{1,0:T(8,128)}) %reduce-scatter.7.cloned.1.call-update) | async-done | bytes 524304
  584.6 41.9 %reduce-scatter.5.cloned.1.call-done = f32[32,1024]{1,0:T(8,128)} async-done(((f32[256,1024]{1,0:T(8,128)}), f32[32,1024]{1,0:T(8,128)}) %reduce-scatter.5.cloned.1.call-update) | async-done | bytes 131088 | tf_op jit(solution)/shard_map/reduce_scatter | solution.py:129
  (166 shorter events, 135.0 us)
Async XLA Ops:
  7.2 54.0 %all-gather.4.cloned.1.call-start = ((), (), s32[]{:S(2)}) async-start(), calls=%async_computation.2 | async-start | bytes 2228224 | tf_op jit(solution)/shard_map/all_gather | solution.py:35
  7.9 481.5 %all-reduce.2.cloned.1.call-start = ((), (), s32[]{:S(2)}) async-start(), calls=%async_computation.4 | async-start | bytes 8388608 | tf_op jit(solution)/shard_map/psum | solution.py:137
  8.0 60.7 %copy-start.1 = (bf16[256,1024]{1,0:T(8,128)(2,1)S(1)}, bf16[256,1024]{1,0:T(8,128)(2,1)}, u32[]{:S(2)}) copy-start(bf16[256,1024]{1,0:T(8,128)(2,1)} %param.13) | copy-start | bytes 1572868
  68.6 91.6 %copy-start.4 = (bf16[512,1024]{1,0:T(8,128)(2,1)S(1)}, bf16[512,1024]{1,0:T(8,128)(2,1)}, u32[]{:S(2)}) copy-start(bf16[512,1024]{1,0:T(8,128)(2,1)} %param.17) | copy-start | bytes 3145732
  250.0 80.9 %copy-start.3 = (bf16[512,1024]{1,0:T(8,128)(2,1)S(1)}, bf16[512,1024]{1,0:T(8,128)(2,1)}, u32[]{:S(2)}) copy-start(bf16[512,1024]{1,0:T(8,128)(2,1)} %param.16) | copy-start | bytes 3145732
  330.9 10.5 %copy-start = (f32[256,1024]{1,0:T(8,128)}, f32[256,1024]{1,0:T(8,128)S(1)}, u32[]{:S(2)}) copy-start(f32[256,1024]{1,0:T(8,128)S(1)} %get-tuple-element.497) | copy-start | bytes 3145732
  341.4 1.6 copy-start.2
  341.4 241.3 %reduce-scatter.7.cloned.1.call-start = ((), (), s32[]{:S(2)}) async-start(), calls=%async_computation.5 | async-start | bytes 4718592
  358.3 268.3 %reduce-scatter.5.cloned.1.call-start = ((), (), s32[]{:S(2)}) async-start(), calls=%async_computation.3 | async-start | bytes 1179648 | tf_op jit(solution)/shard_map/reduce_scatter | solution.py:129
Sparse Core Ops, SparseCore 0:
  10.4 50.7 all-gather.3
  341.6 147.7 all-reduce.1
  491.8 90.8 reduce-scatter.6
  585.5 40.9 reduce-scatter.4
where the time goes:
time: 636 us; the launch traced here: 633 us
  waiting for transfers between devices  319 us (50%)
  matrix products  169 us (27%)
  blocking collectives  75.5 us (12%)
  loops' own time  26.6 us (4%)
  local copies, waits for them, and re-layouts  25.9 us (4%)
  between operations  13.9 us (2%)
    psum x1, waiting for transfers between devices, local(): lax.psum(lax.dot_general(grad_kv, up_both, contract_cols, preferred_eleme...  131 us
    unnamed x5, waiting for transfers between devices  92.9 us
    dot_general x24, matrix products, masked_scores(): lax.dot_general(query_head.astype(jnp.float32), key_head, contract_cols,...  63.4 us
    all_gather x2, blocking collectives, joined(): gathered = jax.tree.map(lambda a: lax.all_gather(a, axis), part)  56.4 us
    all_gather x1, waiting for transfers between devices, local(): block = lax.all_gather(latent, 'head', axis=0, tiled=True)  53.2 us
    reduce_scatter x1, waiting for transfers between devices, local(): lax.psum_scatter(query_acc, 'ctx', scatter_dimension=0, tiled=True)  41.9 us
    dot_general x16, matrix products, product_scores(): lax.dot_general(grad_head, value_head, contract_cols, preferred_element_t...  25.1 us
    another operation x1, loops' own time, local(): deltas = lax.psum(lax.map(local_delta, head_ids), 'ctx')  21 us
  transfers between devices with their start and end apart: 4, of which 4 were waited for; matrix products, arithmetic and copies ran while one was open for 3% of the time, Pallas kernels for 0%

commit v1 on v0

--- a/solution.py
+++ b/solution.py
@@ -32,7 +32,10 @@
     query_count = queries.shape[0]
     contract_cols = (((1,), (1,)), ((), ()))
     contract_rows = (((0,), (0,)), ((), ()))
-    block = lax.all_gather(latent, "head", axis=0, tiled=True)
+    size = lax.axis_size("head")
+    pieces = jnp.stack([latent for _ in range(size)])
+    pieces = lax.all_to_all(pieces, "head", split_axis=0, concat_axis=0)
+    block = jnp.concatenate(pieces, axis=0)
     key_rows = block.shape[0]
     total_len = key_rows * lax.axis_size("ctx")
     first_key = lax.axis_index("ctx") * key_rows

time: 636 us -> 520 us (0.82)
  waiting for transfers between devices: 319 us -> 187 us
  starting transfers between devices: 0.16 us -> 8.26 us
    unnamed x5 -> x4, waiting for transfers between devices: 92.9 us -> 0.57 us
    all_gather x1 -> x0, waiting for transfers between devices: 53.2 us -> none  [local(): block = lax.all_gather(latent, 'head', axis=0, tiled=True)]
    all_to_all x0 -> x1, waiting for transfers between devices: none -> 29.1 us  [local(): pieces = lax.all_to_all(pieces, 'head', split_axis=0, concat_axis=0)]
    reduce_scatter x1, waiting for transfers between devices: 41.9 us -> 15.6 us  [local(): lax.psum_scatter(query_acc, 'ctx', scatter_dimension=0, tiled=True)]
    psum x1, waiting for transfers between devices: 131 us -> 142 us  [local(): lax.psum(lax.dot_general(grad_kv, up_both, contract_cols, preferred_eleme...]
    all_to_all x0 -> x1, starting transfers between devices: none -> 8.13 us  [local(): pieces = lax.all_to_all(pieces, 'head', split_axis=0, concat_axis=0)]
    dot_general x8, matrix products: 11 us -> 17.7 us  [accumulate(): lax.dot_general(grad_scores, query_head, contract_rows, preferred_element...]
  transfers between devices with their start and end apart: 4 -> 4, of which waited for: 4 -> 3; matrix products, arithmetic and copies ran while one was open for 3% -> 4% of each run, Pallas kernels for 0% -> 0%
where the time goes in v1:
time: 520 us; the launch traced here: 517 us
  waiting for transfers between devices  187 us (36%)
  matrix products  173 us (33%)
  blocking collectives  76 us (15%)
  loops' own time  26.6 us (5%)
  local copies, waits for them, and re-layouts  26.4 us (5%)
  between operations  15.6 us (3%)
  starting transfers between devices  8.26 us (2%)
    psum x1, waiting for transfers between devices, local(): lax.psum(lax.dot_general(grad_kv, up_both, contract_cols, preferred_eleme...  142 us
    dot_general x24, matrix products, masked_scores(): lax.dot_general(query_head.astype(jnp.float32), key_head, contract_cols,...  64.2 us
    all_gather x2, blocking collectives, joined(): gathered = jax.tree.map(lambda a: lax.all_gather(a, axis), part)  56.4 us
    all_to_all x1, waiting for transfers between devices, local(): pieces = lax.all_to_all(pieces, 'head', split_axis=0, concat_axis=0)  29.1 us
    dot_general x16, matrix products, product_scores(): lax.dot_general(grad_head, value_head, contract_cols, preferred_element_t...  25.1 us
    another operation x1, loops' own time, local(): deltas = lax.psum(lax.map(local_delta, head_ids), 'ctx')  21 us
    psum x1, blocking collectives, local(): deltas = lax.psum(lax.map(local_delta, head_ids), 'ctx')  19.5 us
    dot_general x8, matrix products, accumulate(): jnp.dot(grad_scores.astype(jnp.float32), key_head, precision=lax.Precisio...  18.1 us
  transfers between devices with their start and end apart: 4, of which 3 were waited for; matrix products, arithmetic and copies ran while one was open for 4% of the time, Pallas kernels for 0%

profile of v1, /device:TPU:0, one launch (start us, length us, event | category | flops | bytes accessed | tf_op | source)
XLA Modules:
  0.0 517.1 jit_solution(13181663316069778548)
XLA Ops:
  10.4 8.1 %all-to-all-start = ((bf16[16,128,512]{2,1,0:T(8,128)(2,1)}), bf16[16,128,512]{2,1,0:T(8,128)(2,1)S(1)}, u32[]{:S(2)}, u32[]{:S(2)}) async-start(bf16[16,128,512]{2,1,0:T(8,128)(2,1)} %stack.2), calls=%async_computation | async-start | bytes 4194304 | tf_op jit(solution)/shard_map/all_to_all | solution.py:37
  18.7 29.1 %all-to-all-done = bf16[16,128,512]{2,1,0:T(8,128)(2,1)S(1)} async-done(((bf16[16,128,512]{2,1,0:T(8,128)(2,1)}), bf16[16,128,512]{2,1,0:T(8,128)(2,1)S(1)}, u32[]{:S(2)}, u32[]{:S(2)}) %all-to-all-start) | async-done | bytes 2097184 | tf_op jit(solution)/shard_map/all_to_all | solution.py:37
  47.8 4.3 convolution_convert_fusion.2
  52.0 5.6 %fusion.52 = f32[2048,1024]{1,0:T(8,128)} fusion(bf16[2048,512]{1,0:T(8,128)(2,1)S(1)} %bitcast.64, bf16[512,1024]{1,0:T(8,128)(2,1)S(1)} %copy-done.1), kind=kOutput, calls=%fused_computation.71 | convolution fusion | flops 2147483648 | bytes 11534336 | tf_op jit(solution)/shard_map/dot_general | solution.py:42
  57.6 34.8 %while.60 = (s32[]{:T(128)}, f32[8,256]{1,0:T(8,128)S(1)}, f32[8,256]{1,0:T(8,128)S(1)}, s32[8]{0:T(128)S(1)}, bf16[256,1024]{1,0:T(8,128)(2,1)}, /*index=5*/f32...) while((s32[]{:T(128)}, f32[8,256]{1,0:T(8,128)S(1)}, ...), condition=%wide.region_3.4_spmd.clone, body=%wide.region_0.3_spmd.clone.sunk | while | flops 808451584 | bytes 5326015 | solution.py:84
  92.4 28.3 %all-gather.1 = f32[64,256]{1,0:T(8,128)S(1)} all-gather(f32[8,256]{1,0:T(8,128)S(1)} %get-tuple-element.493), channel_id=3, replica_groups=mesh['ctx'=8,'head'=16] {'ctx'}, dimensions={0}, use_global_device_ids=true | all-gather | bytes 73728 | tf_op jit(solution)/shard_map/all_gather | solution.py:11
  120.7 28.2 %all-gather = f32[64,256]{1,0:T(8,128)S(1)} all-gather(f32[8,256]{1,0:T(8,128)S(1)} %get-tuple-element.492), channel_id=2, replica_groups=mesh['ctx'=8,'head'=16] {'ctx'}, dimensions={0}, use_global_device_ids=true | all-gather | bytes 73728 | tf_op jit(solution)/shard_map/all_gather | solution.py:11
  149.2 60.7 %while.61 = (s32[]{:T(128)}, f32[8,256]{1,0:T(8,128)S(1)}, s32[8]{0:T(128)S(1)}, bf16[256,1024]{1,0:T(8,128)(2,1)}, f32[2048,1024]{1,0:T(8,128)}, /*index=5*/f32...) while((s32[]{:T(128)}, f32[8,256]{1,0:T(8,128)S(1)}, ...), condition=%wide.region_8.9_spmd.clone, body=%wide.region_6.8_spmd.clone.sunk | while | flops 943193856 | bytes 5918977 | solution.py:96
  209.9 19.5 %psum.14 = f32[8,256]{1,0:T(8,128)S(1)} all-reduce(f32[8,256]{1,0:T(8,128)S(1)} %get-tuple-element.496), channel_id=1, replica_groups=mesh['ctx'=8,'head'=16] {'ctx'}, use_global_device_ids=true, to_apply=%region_9.10 | all-reduce | flops 2048 | bytes 16384 | tf_op jit(solution)/shard_map/psum | solution.py:96
  229.5 4.3 broadcast_in_dim.48
  233.8 87.8 %while.62 = (s32[]{:T(128)}, f32[256,1024]{1,0:T(8,128)S(1)}, bf16[2048,2048]{1,0:T(8,128)(2,1)}, bf16[256,1024]{1,0:T(8,128)(2,1)}, f32[2048,1024]{1,0:T(8,128)...) while((s32[]{:T(128)}, f32[256,1024]{1,0:T(8,128)S(1)}, ...), condition=%wide.region_11.12_spmd.clone, body=%wide.region_10.11_spmd.clone.sunk | while | flops 2019033088 | bytes 13522222 | solution.py:130
  233.8 2.7 fusion.102
  244.8 2.7 fusion.102
  255.8 2.7 fusion.102
  266.8 2.7 fusion.102
  277.7 2.7 fusion.102
  288.7 2.7 fusion.102
  299.7 2.7 fusion.102
  310.6 2.7 fusion.102
  321.6 10.8 %fusion.45 = f32[2048,512]{1,0:T(8,128)} fusion(bf16[2048,2048]{1,0:T(8,128)(2,1)} %get-tuple-element.498, bf16[512,1024]{1,0:T(8,128)(2,1)} %param.17, bf16[512,1024]{1,0:T(8,128)(2,1)} %param.16), kind=kOutput, calls=%fused_computation.61 | convolution fusion | flops 4299161600 | bytes 14680064 | tf_op jit(solution)/shard_map/dot_general | solution.py:141
  332.5 9.8 %convolution_bitcast_fusion = f32[512,2048]{0,1:T(8,128)} fusion(bf16[2048,2048]{1,0:T(8,128)(2,1)} %get-tuple-element.498, bf16[2048,512]{1,0:T(8,128)(2,1)S(1)} %bitcast.65), kind=kOutput, calls=%fused_computation.60 | convolution fusion | flops 4294967296 | bytes 14680064 | tf_op jit(solution)/shard_map/dot_general | solution.py:134
  342.3 5.4 %copy.13 = f32[512,2048]{1,0:T(8,128)} copy(f32[512,2048]{0,1:T(8,128)} %convolution_bitcast_fusion) | data formatting | bytes 8388608
  348.3 142.2 %all-reduce.2.cloned.1.call-done = f32[2048,512]{1,0:T(8,128)} async-done(((f32[2048,512]{1,0:T(8,128)}), f32[2048,512]{1,0:T(8,128)}) %all-reduce.2.cloned.1.call-update) | async-done | bytes 4194320 | tf_op jit(solution)/shard_map/psum | solution.py:140
  494.1 15.6 %reduce-scatter.5.cloned.1.call-done = f32[32,1024]{1,0:T(8,128)} async-done(((f32[256,1024]{1,0:T(8,128)}), f32[32,1024]{1,0:T(8,128)}) %reduce-scatter.5.cloned.1.call-update) | async-done | bytes 131088 | tf_op jit(solution)/shard_map/reduce_scatter | solution.py:132
  (162 shorter events, 142.2 us)
Async XLA Ops:
  10.4 37.3 %copy-start.2 = (bf16[512,1024]{1,0:T(8,128)(2,1)S(1)}, bf16[512,1024]{1,0:T(8,128)(2,1)}, u32[]{:S(2)}) copy-start(bf16[512,1024]{1,0:T(8,128)(2,1)} %param.17) | copy-start | bytes 3145732
  10.4 37.3 %all-to-all-start = ((bf16[16,128,512]{2,1,0:T(8,128)(2,1)}), bf16[16,128,512]{2,1,0:T(8,128)(2,1)S(1)}, u32[]{:S(2)}, u32[]{:S(2)}) async-start(bf16[16,128,512]{2,1,0:T(8,128)(2,1)} %stack.2), calls=%async_computation | async-start | bytes 4194304 | tf_op jit(solution)/shard_map/all_to_all | solution.py:37
  18.6 472.0 %all-reduce.2.cloned.1.call-start = ((), (), s32[]{:S(2)}) async-start(), calls=%async_computation.4 | async-start | bytes 8388608 | tf_op jit(solution)/shard_map/psum | solution.py:140
  47.8 4.3 copy-start.1
  321.6 10.8 %copy-start = (f32[256,1024]{1,0:T(8,128)}, f32[256,1024]{1,0:T(8,128)S(1)}, u32[]{:S(2)}) copy-start(f32[256,1024]{1,0:T(8,128)S(1)} %get-tuple-element.497) | copy-start | bytes 3145732
  332.5 159.8 %reduce-scatter.7.cloned.1.call-start = ((), (), s32[]{:S(2)}) async-start(), calls=%async_computation.5 | async-start | bytes 4718592
  347.7 161.9 %reduce-scatter.5.cloned.1.call-start = ((), (), s32[]{:S(2)}) async-start(), calls=%async_computation.3 | async-start | bytes 1179648 | tf_op jit(solution)/shard_map/reduce_scatter | solution.py:132
Sparse Core Ops, SparseCore 0:
  332.6 157.9 all-reduce.1
Sparse Core Ops, SparseCore 1:
  347.8 116.6 reduce-scatter.6
  467.3 42.3 reduce-scatter.4
